TPU v7x, 256 devices: a whole 4x4x8 slice. The times are simulated.
256 devices in a mesh: seq: 32 (over y, x, core), exp: 8 (over z).
Axes of the slice: x: 4, y: 4, z: 8, core: 2. Of those that a mesh axis runs over, the one named last changes fastest.
Arguments:
- queries: bfloat16 [4096, 7168], P('seq', 'exp'), may hold values from -8 to 8
- keys: bfloat16 [4096, 7168], P('seq', 'exp'), may hold values from -8 to 8
- values: bfloat16 [4096, 7168], P('seq', 'exp'), may hold values from -34 to 34
- branch_gates: float32 [4096, 2, 56], P('seq', None, 'exp'), may hold values from 0.1 to 1
- block_choice: int32 [64, 8], P('seq'), may hold values from 0 to 14, as said below
- norm_gain: float32 [7168], P('exp'), may hold values from 0.5 to 1.5
- expert_ids: int32 [4096, 8], P('seq'), may hold values from 0 to 31, all different within a row; in each aligned block of 128 rows (0 to 127, 128 to 255, ...) at most 40 rows name the same one
- route_scores: float32 [4096, 8], P('seq'), may hold values from 0.05 to 1
- w_gate_up: bfloat16 [32, 7168, 2, 1536], P('seq', 'exp'), may hold values from -0.0625 to 0.0625
- w_down: bfloat16 [32, 1536, 7168], P('seq', None, 'exp'), may hold values from -0.15625 to 0.15625
Outputs:
- mixed: bfloat16 [4096, 7168], P('seq', 'exp')
Inputs may be any that keep to these rules, and one draw needn't show every extreme that they name: `block_choice`: each row holds offset 0 and 7 other distinct offsets. `expert_ids`: each row names 8 different experts; within each aligned block of 128 rows (the rows of one index of seq) no expert is named more than 40 times, and that many is reached.
All inputs are finite; a program needn't handle non-finite values.
Results may differ from a plain program's by a relative error of at most 0.029.
Values may be sent and summed in bfloat16 or wider, within the bound.
No kernel may reach another device: no remote copies, remote signals or barrier semaphores. Data moves between devices by JAX's collectives and lax.ppermute only.
A program may use at most 128 MiB of HBM per device.

v0:
```python
import jax
import jax.numpy as jnp
from jax import lax
from jax.sharding import PartitionSpec as P

HD = 128
D = 7168
BLOCK = 64
WINDOW = 15
EPSILON = 1e-06
ROUTE_SCALE = 2.5
MASKED_SCORE = -1e30


def copy_for_each(shard, axis):
    copies = jnp.broadcast_to(shard, (lax.axis_size(axis), *shard.shape))
    return lax.all_to_all(copies, axis, split_axis=0, concat_axis=0, tiled=True)


def joined_along(parts, dim):
    parts = jnp.moveaxis(parts, 0, dim)
    shape = parts.shape
    return parts.reshape(*shape[:dim], shape[dim] * shape[dim + 1], *shape[dim + 2 :])


def collect(shard, axis, dim):
    parts = copy_for_each(shard, axis)
    return joined_along(parts, dim)


def passed_along(shard, axis, by):
    peers = lax.axis_size(axis)
    pairs = [(i, i + by) for i in range(peers) if 0 <= i + by < peers]
    return lax.ppermute(shard, axis, pairs)


def local(
    queries,
    keys,
    values,
    branch_gates,
    block_choice,
    norm_gain,
    expert_ids,
    route_scores,
    w_gate_up,
    w_down,
):
    tokens_here = queries.shape[0]
    features = queries.shape[1]
    heads_here = features // HD
    blocks_here = tokens_here // BLOCK
    device_row = lax.axis_index("seq")
    seq_devices = lax.axis_size("seq")
    score_scale = HD ** (-0.5)
    query_heads = queries.reshape(tokens_here, heads_here, HD)
    positions = jnp.arange(tokens_here, dtype=jnp.int32)
    query_block = device_row * blocks_here + positions // BLOCK
    query_pos = device_row * tokens_here + positions
    chosen = jnp.repeat(block_choice, BLOCK, axis=0)
    local_kv = jnp.stack([keys, values])
    pooled = jnp.mean(
        local_kv.astype(jnp.float32).reshape(2, blocks_here, BLOCK, features), axis=2
    ).astype(jnp.bfloat16)
    everyone = collect(pooled, "seq", 1)
    all_blocks = everyone.shape[1]
    pooled_keys = everyone[0].reshape(all_blocks, heads_here, HD)
    pooled_values = everyone[1].reshape(all_blocks, heads_here, HD)
    scores = (
        jnp.einsum("qhd,chd->hqc", query_heads, pooled_keys, preferred_element_type=jnp.float32)
        * score_scale
    )
    earlier = jnp.arange(all_blocks, dtype=jnp.int32)[None, :] < query_block[:, None]
    masked = jnp.where(earlier[None], scores, MASKED_SCORE)
    row_max = jnp.max(masked, axis=2, keepdims=True)
    row_max = jnp.where(row_max > 0.5 * MASKED_SCORE, row_max, 0.0)
    weights = jnp.where(earlier[None], jnp.exp(scores - row_max), 0.0)
    weight_sum = jnp.sum(weights, axis=2)
    coarse_out = jnp.einsum(
        "hqc,chd->hqd",
        weights.astype(jnp.bfloat16),
        pooled_values,
        preferred_element_type=jnp.float32,
    )
    coarse_out = coarse_out / jnp.maximum(weight_sum, 1.0)[..., None]

    def attend(carried, kv_piece, first_block):
        running_max, denominator, numerator = carried
        key_count = kv_piece.shape[1]
        key_heads = kv_piece[0].reshape(key_count, heads_here, HD)
        value_heads = kv_piece[1].reshape(key_count, heads_here, HD)
        key_offsets = jnp.arange(key_count, dtype=jnp.int32)
        key_block = first_block + key_offsets // BLOCK
        key_pos = first_block * BLOCK + key_offsets
        block_gap = query_block[:, None] - key_block[None, :]
        picked = jnp.any(chosen[:, :, None] == block_gap[:, None, :], axis=1)
        allowed = picked & (key_block >= 0)[None, :] & (key_pos[None, :] <= query_pos[:, None])
        piece_scores = (
            jnp.einsum("qhd,khd->hqk", query_heads, key_heads, preferred_element_type=jnp.float32)
            * score_scale
        )
        piece_masked = jnp.where(allowed[None], piece_scores, MASKED_SCORE)
        updated_max = jnp.maximum(running_max, jnp.max(piece_masked, axis=2))
        piece_weights = jnp.where(
            allowed[None], jnp.exp(piece_scores - updated_max[..., None]), 0.0
        )
        rescale = jnp.exp(running_max - updated_max)
        denominator = denominator * rescale + jnp.sum(piece_weights, axis=2)
        numerator = numerator * rescale[..., None] + jnp.einsum(
            "hqk,khd->hqd",
            piece_weights.astype(jnp.bfloat16),
            value_heads,
            preferred_element_type=jnp.float32,
        )
        return (updated_max, denominator, numerator)

    carried = (
        jnp.full((heads_here, tokens_here), MASKED_SCORE, jnp.float32),
        jnp.zeros((heads_here, tokens_here), jnp.float32),
        jnp.zeros((heads_here, tokens_here, HD), jnp.float32),
    )
    carried = attend(carried, local_kv, device_row * blocks_here)
    reach_devices = min(seq_devices - 1, (WINDOW - 2) // blocks_here + 1)
    gathered = local_kv
    stride = 1
    while stride <= reach_devices:
        incoming = passed_along(gathered, "seq", stride)
        carried = attend(carried, incoming, (device_row - 2 * stride + 1) * blocks_here)
        gathered = jnp.concatenate([incoming, gathered], axis=1)
        stride = stride * 2
    fine_out = carried[2] / carried[1][..., None]
    mixed_heads = (
        jnp.transpose(branch_gates[:, 0, :])[..., None] * coarse_out
        + jnp.transpose(branch_gates[:, 1, :])[..., None] * fine_out
    )
    hidden_state = (
        jnp.transpose(mixed_heads, (1, 0, 2)).reshape(tokens_here, features).astype(jnp.bfloat16)
    )
    routes_per = expert_ids.shape[1]
    capacity = 5 * tokens_here * routes_per // (4 * seq_devices)
    flat_ids = expert_ids.reshape(-1)
    onehot = (flat_ids[:, None] == jnp.arange(seq_devices, dtype=jnp.int32)[None, :]).astype(
        jnp.int32
    )
    slot_index = jnp.sum((jnp.cumsum(onehot, axis=0) - 1) * onehot, axis=1)
    destination = flat_ids * capacity + slot_index
    rows_of = jnp.arange(tokens_here * routes_per, dtype=jnp.int32) // routes_per
    outgoing = (
        jnp.zeros((seq_devices * capacity, features), jnp.bfloat16)
        .at[destination]
        .set(hidden_state[rows_of])
    )
    outgoing = outgoing.reshape(seq_devices, capacity, features)
    arrived = lax.all_to_all(outgoing, "seq", split_axis=0, concat_axis=0, tiled=True)
    sources = arrived.shape[0]
    slots = arrived.shape[1]
    wide_rows = arrived.reshape(sources * slots, features).astype(jnp.float32)
    squares = jnp.sum(wide_rows * wide_rows, axis=1)
    normed = (wide_rows * norm_gain).astype(jnp.bfloat16)
    partials = jnp.einsum("rd,dgh->rgh", normed, w_gate_up[0], preferred_element_type=jnp.float32)
    spread = jnp.broadcast_to(squares[:, None], (squares.shape[0], lax.axis_size("exp")))
    summed = lax.psum_scatter(
        partials.astype(jnp.bfloat16), "exp", scatter_dimension=2, tiled=True
    ).astype(jnp.float32)
    square_share = lax.psum_scatter(
        spread.astype(jnp.bfloat16), "exp", scatter_dimension=1, tiled=True
    ).astype(jnp.float32)
    row_scale = lax.rsqrt(square_share[:, 0] / D + EPSILON)[:, None]
    activated = (jax.nn.silu(summed[:, 0] * row_scale) * (summed[:, 1] * row_scale)).astype(
        jnp.bfloat16
    )
    down_rows = w_down[0]
    result = jnp.dot(
        lax.all_gather(activated, "exp", axis=1, tiled=True),
        down_rows,
        preferred_element_type=jnp.float32,
    )
    results_here = result.astype(jnp.bfloat16).reshape(sources, slots, features)
    returned = lax.all_to_all(results_here, "seq", split_axis=0, concat_axis=0, tiled=True)
    flattened = returned.reshape(seq_devices * capacity, features)
    picked_rows = flattened[destination].reshape(tokens_here, routes_per, features)
    route_weight = ROUTE_SCALE * route_scores / jnp.sum(route_scores, axis=1, keepdims=True)
    routed = jnp.einsum("tk,tkd->td", route_weight, picked_rows.astype(jnp.float32))
    return (hidden_state.astype(jnp.float32) + routed).astype(jnp.bfloat16)


def solution(mesh):
    placed = (
        P("seq", "exp"),
        P("seq", "exp"),
        P("seq", "exp"),
        P("seq", None, "exp"),
        P("seq", None),
        P("exp"),
        P("seq", None),
        P("seq", None),
        P("seq", "exp", None, None),
        P("seq", None, "exp"),
    )
    return jax.shard_map(
        local, mesh=mesh, in_specs=placed, out_specs=P("seq", "exp"), check_vma=False
    )
```

profile of v0, /device:TPU:1, one launch (start us, length us, event | category | flops | bytes accessed | tf_op | source)
XLA Modules:
  0.0 424.2 jit_solution(7948450174983795036)
XLA Ops:
  6.5 1.2 copy.98
  7.8 1.1 copy.102
  8.9 0.8 pad_maximum_fusion
  9.8 4.5 %collective-permute-start = (bf16[2,128,896]{1,2,0:T(8,128)(2,1)}, bf16[2,128,896]{1,2,0:T(8,128)(2,1)}, u32[]{:S(2)}, u32[]{:S(2)}) collective-permute-start(bf16[2,128,896]{1,2,0:T(8,128)(2,1)} %pad_maximum_fusion), channel_id=1, source_target_pairs={{0,8},{8,16},{16,24},{24,32},{32,40},{40,48},{48,56},{56,64},{64,7... | collective-permute-start | bytes 1376264 | tf_op jit(solution)/shard_map/ppermute | solution.py:34
  14.3 1.0 convert_reduce_fusion
  15.3 0.8 broadcast_in_dim.167
  16.1 7.0 %all-to-all-start = ((bf16[32,2,2,896]{3,2,1,0:T(2,128)(2,1)}), bf16[32,2,2,896]{3,2,1,0:T(2,128)(2,1)}, u32[]{:S(2)}, u32[]{:S(2)}) async-start(bf16[32,2,2,896]{3,2,1,0:T(2,128)(2,1)} %broadcast_in_dim.167), calls=%async_computation | async-start | bytes 458752 | tf_op jit(solution)/shard_map/all_to_all | solution.py:17
  24.9 0.7 broadcast_subtract_fusion.2
  26.4 1.3 compare_reduce_fusion
  27.7 1.0 compare_reduce_fusion.1
  30.8 15.6 %reduce-window.6 = s32[32,8,128]{2,1,0:T(8,128)S(1)} reduce-window(s32[32,8,128]{2,1,0:T(8,128)} %fusion.62, s32[]{:T(128)} %constant.123.clone.1), window={size=1x1x128 pad=0_0x0_0x127_0}, to_apply=%region_16.17 | reduce-window | flops 4161536 | bytes 262148 | tf_op jit(solution)/shard_map/reduce-window
  46.4 0.8 slice.70
  47.1 1.0 copy.122
  48.7 0.7 copy.123
  49.5 0.7 add_add_fusion
  50.2 1.2 compare_reduce_fusion.3
  51.5 1.6 compare_and_fusion
  53.1 1.5 compare_and_fusion.1
  54.5 0.8 compare_and_fusion.3
  55.3 1.3 broadcast_multiply_fusion
  56.6 0.7 eq.89
  57.4 1.1 copy.92
  58.5 0.7 copy.97
  59.2 1.0 copy.114
  60.2 0.9 copy.110
  61.1 1.3 copy.157
  62.4 1.3 copy.156
  63.6 1.4 copy.119
  65.0 1.5 mul.235
  66.5 0.9 fusion.61
  67.5 1.3 compare_select_fusion.1
  68.8 2.0 maximum_maximum_fusion.1
  70.8 4.2 collective-permute-start.1
  75.6 1.6 select_reduce_fusion.2
  77.8 1.8 fusion.97
  79.7 1.6 reshape_squeeze.24
  81.3 12.4 %collective-permute-done.1 = bf16[2,256,896]{1,2,0:T(8,128)(2,1)} collective-permute-done((bf16[2,256,896]{1,2,0:T(8,128)(2,1)}, bf16[2,256,896]{1,2,0:T(8,128)(2,1)}, u32[]{:S(2)}, u32[]{:S(2)}) %collective-permute-start.1) | collective-permute-done | bytes 917536 | tf_op jit(solution)/shard_map/ppermute | solution.py:34
  93.7 2.7 maximum_maximum_fusion
  96.4 6.8 %collective-permute-start.2 = (bf16[2,512,896]{1,2,0:T(8,128)(2,1)}, bf16[2,512,896]{1,2,0:T(8,128)(2,1)}, u32[]{:S(2)}, u32[]{:S(2)}) collective-permute-start(bf16[2,512,896]{1,2,0:T(8,128)(2,1)} %maximum_maximum_fusion), channel_id=1, source_target_pairs={{0,32},{8,40},{16,48},{24,56},{32,64},{40,72},{48,80},{56,88},{64,... | collective-permute-start | bytes 5505032 | tf_op jit(solution)/shard_map/ppermute | solution.py:34
  103.2 0.8 select_reduce_fusion.3
  104.1 1.6 reshape_squeeze.25
  105.7 0.7 compare_select_fusion.2
  106.4 0.7 fusion.58
  107.1 1.2 fusion.24
  108.3 1.1 fusion.96
  109.7 1.2 fusion.95
  111.3 29.2 %collective-permute-done.2 = bf16[2,512,896]{1,2,0:T(8,128)(2,1)} collective-permute-done((bf16[2,512,896]{1,2,0:T(8,128)(2,1)}, bf16[2,512,896]{1,2,0:T(8,128)(2,1)}, u32[]{:S(2)}, u32[]{:S(2)}) %collective-permute-start.2) | collective-permute-done | bytes 1835040 | tf_op jit(solution)/shard_map/ppermute | solution.py:34
  140.4 1.6 fusion.94
  145.7 13.9 %scatter_custom_fusion = bf16[1280,896]{1,0:T(8,128)(2,1)} fusion(s32[1024]{0:T(1024)S(1)} %bitcast.247, bf16[128,896]{1,0:T(8,128)(2,1)S(1)} %copy.118, s32[1024]{0:T(1024)} %broadcast_clamp_fusion.1, bf16[]{:T(256)} %constant.138.clone.1), kind=kCustom, calls=%fused_computation.20 | custom fusion | bytes 2294272 | tf_op jit(solution)/shard_map/scatter | solution.py:151
  159.5 41.4 %all_to_all.15 = bf16[32,40,896]{2,1,0:T(8,128)(2,1)S(1)} all-to-all(bf16[32,40,896]{2,1,0:T(8,128)(2,1)} %bitcast.216), channel_id=1, replica_groups=mesh['seq'=32,'exp'=8] {'seq'}, dimensions={0} | all-to-all | bytes 4587520 | tf_op jit(solution)/shard_map/all_to_all | solution.py:154
  200.9 0.8 fusion.2
  201.7 16.0 %convolution_convert_fusion = bf16[1280,2,1536]{0,2,1:T(8,128)(2,1)} fusion(bf16[1280,896,1]{1,0,2:T(8,128)(2,1)S(1)} %bitcast.232, bf16[896,2,1536]{2,1,0:T(2,128)(2,1)} %bitcast.252), kind=kOutput, calls=%fused_computation.3 | convolution fusion | flops 7050362880 | bytes 15663104 | tf_op jit(solution)/shard_map/rd,dgh->rgh/dot_general | solution.py:160
  219.0 29.2 %all-reduce = bf16[1280,8]{0,1:T(8,128)(2,1)S(1)} all-reduce(bf16[1280,8]{0,1:T(8,128)(2,1)S(1)} %broadcast_in_dim.186), channel_id=3, replica_groups=mesh['seq'=32,'exp'=8] {'exp'}, use_global_device_ids=true, to_apply=%region_22.23.clone | all-reduce | flops 10240 | bytes 40960
  248.2 0.7 rsqrt_reduce_fusion
  248.8 58.5 %reduce-scatter.2.cloned.1.call-done = bf16[1280,2,192]{0,2,1:T(8,128)(2,1)} async-done(((bf16[1280,2,1536]{0,2,1:T(8,128)(2,1)}), bf16[1280,2,192]{0,2,1:T(8,128)(2,1)}) %reduce-scatter.2.cloned.1.call-update) | async-done | bytes 983056 | tf_op jit(solution)/shard_map/reduce_scatter | solution.py:162
  307.3 1.3 convert_element_type.88
  308.7 1.1 fusion.32
  309.8 50.7 %all-gather.2.cloned.1.call-done = bf16[1280,1536]{0,1:T(8,128)(2,1)} async-done(((bf16[1280,192]{0,1:T(8,128)(2,1)}), bf16[1280,1536]{0,1:T(8,128)(2,1)}) %all-gather.2.cloned.1.call-update) | async-done | bytes 3932176 | tf_op jit(solution)/shard_map/all_gather | solution.py:174
  360.4 7.6 %convolution_convert_fusion.1 = bf16[1280,896]{1,0:T(8,128)(2,1)} fusion(bf16[1280,1536]{0,1:T(8,128)(2,1)} %all-gather.2.cloned.1.call-done, bf16[1,1536,896]{2,1,0:T(8,128)(2,1)S(1)} %copy-done), kind=kOutput, calls=%fused_computation.9 | convolution fusion | flops 3524362240 | bytes 8978432 | tf_op jit(solution)/shard_map/dot_general | solution.py:173
  368.0 7.9 %all-to-all-start.2 = ((bf16[32,40,896]{2,1,0:T(8,128)(2,1)}), bf16[32,40,896]{2,1,0:T(8,128)(2,1)}, u32[]{:S(2)}, u32[]{:S(2)}) async-start(bf16[32,40,896]{2,1,0:T(8,128)(2,1)} %bitcast.231), calls=%async_computation.3 | async-start | bytes 4587520 | tf_op jit(solution)/shard_map/all_to_all | solution.py:179
  376.1 30.6 %all-to-all-done.2 = bf16[32,40,896]{2,1,0:T(8,128)(2,1)} async-done(((bf16[32,40,896]{2,1,0:T(8,128)(2,1)}), bf16[32,40,896]{2,1,0:T(8,128)(2,1)}, u32[]{:S(2)}, u32[]{:S(2)}) %all-to-all-start.2) | async-done | bytes 2293792 | tf_op jit(solution)/shard_map/all_to_all | solution.py:179
  406.7 7.7 %gather_fusion = bf16[1024,896]{1,0:T(8,128)(2,1)} fusion(bf16[1280,896]{1,0:T(8,128)(2,1)} %bitcast.50, s32[1024]{0:T(1024)S(1)} %broadcast_clamp_fusion), kind=kCustom, calls=%fused_computation.1 | custom fusion | bytes 3674112 | tf_op jit(solution)/shard_map/gather | solution.py:181
  414.4 2.2 fusion.4
  416.6 0.7 fusion.42
  (87 shorter events, 12.3 us)
Async XLA Ops:
  6.5 353.9 %copy-start = (bf16[1,1536,896]{2,1,0:T(8,128)(2,1)S(1)}, bf16[1,1536,896]{2,1,0:T(8,128)(2,1)}, u32[]{:S(2)}) copy-start(bf16[1,1536,896]{2,1,0:T(8,128)(2,1)} %param.19) | copy-start | bytes 8257540
  6.5 7.7 %copy-start.2 = (bf16[128,896]{1,0:T(8,128)(2,1)S(1)}, bf16[128,896]{1,0:T(8,128)(2,1)}, u32[]{:S(2)}) copy-start(bf16[128,896]{1,0:T(8,128)(2,1)} %param.12) | copy-start | bytes 688132
  6.5 19.8 %copy-start.16 = (s32[2,8]{1,0:T(2,128)S(1)}, s32[2,8]{1,0:T(2,128)}, u32[]{:S(2)}) copy-start(s32[2,8]{1,0:T(2,128)} %param.14) | copy-start | bytes 196
  7.8 21.5 %copy-start.13 = (f32[128,2,7]{0,1,2:T(2,128)S(1)}, f32[128,2,7]{0,1,2:T(2,128)}, u32[]{:S(2)}) copy-start(f32[128,2,7]{0,1,2:T(2,128)} %param.13) | copy-start | bytes 21508
  7.8 22.1 %copy-start.10 = (s32[128,8]{0,1:T(8,128)S(1)}, s32[128,8]{0,1:T(8,128)}, u32[]{:S(2)}) copy-start(s32[128,8]{0,1:T(8,128)} %param.16) | copy-start | bytes 12292
  9.8 59.0 %collective-permute-start = (bf16[2,128,896]{1,2,0:T(8,128)(2,1)}, bf16[2,128,896]{1,2,0:T(8,128)(2,1)}, u32[]{:S(2)}, u32[]{:S(2)}) collective-permute-start(bf16[2,128,896]{1,2,0:T(8,128)(2,1)} %pad_maximum_fusion), channel_id=1, source_target_pairs={{0,8},{8,16},{16,24},{24,32},{32,40},{40,48},{48,56},{56,64},{64,7... | collective-permute-start | bytes 1376264 | tf_op jit(solution)/shard_map/ppermute | solution.py:34
  16.1 61.7 %all-to-all-start = ((bf16[32,2,2,896]{3,2,1,0:T(2,128)(2,1)}), bf16[32,2,2,896]{3,2,1,0:T(2,128)(2,1)}, u32[]{:S(2)}, u32[]{:S(2)}) async-start(bf16[32,2,2,896]{3,2,1,0:T(2,128)(2,1)} %broadcast_in_dim.167), calls=%async_computation | async-start | bytes 458752 | tf_op jit(solution)/shard_map/all_to_all | solution.py:17
  23.1 284.2 %reduce-scatter.2.cloned.1.call-start = ((), (), s32[]{:S(2)}) async-start(), calls=%async_computation.4 | async-start | bytes 8847360 | tf_op jit(solution)/shard_map/reduce_scatter | solution.py:162
  23.2 3.1 copy-start.8
  66.5 8.5 %copy-start.9 = (s32[128]{0:T(128)S(1)}, s32[128]{0:T(128)}, u32[]{:S(2)}) copy-start(s32[128]{0:T(128)} %copy-done.8) | copy-start | bytes 1540
  66.5 9.1 %copy-start.4 = (pred[128,128]{0,1:T(8,128)(4,1)S(1)}, pred[128,128]{0,1:T(8,128)(4,1)}, u32[]{:S(2)}) copy-start(pred[128,128]{0,1:T(8,128)(4,1)} %copy.97) | copy-start | bytes 49156
  70.8 22.9 %collective-permute-start.1 = (bf16[2,256,896]{1,2,0:T(8,128)(2,1)}, bf16[2,256,896]{1,2,0:T(8,128)(2,1)}, u32[]{:S(2)}, u32[]{:S(2)}) collective-permute-start(bf16[2,256,896]{1,2,0:T(8,128)(2,1)} %maximum_maximum_fusion.1), channel_id=1, source_target_pairs={{0,16},{8,24},{16,32},{24,40},{32,48},{40,56},{48,64},{56,72},{64,... | collective-permute-start | bytes 2752520 | tf_op jit(solution)/shard_map/ppermute | solution.py:34
  81.3 21.9 %copy-start.3 = (bf16[64,7,128]{2,1,0:T(8,128)(2,1)S(1)}, bf16[64,7,128]{2,1,0:T(8,128)(2,1)}, u32[]{:S(2)}) copy-start(bf16[64,7,128]{2,1,0:T(8,128)(2,1)} %reshape_squeeze.24) | copy-start | bytes 344068
  81.3 21.9 %copy-start.6 = (pred[128,64]{0,1:T(8,128)(4,1)S(1)}, pred[128,64]{0,1:T(8,128)(4,1)}, u32[]{:S(2)}) copy-start(pred[128,64]{0,1:T(8,128)(4,1)} %iota_compare_fusion.2) | copy-start | bytes 24580
  96.4 44.0 %collective-permute-start.2 = (bf16[2,512,896]{1,2,0:T(8,128)(2,1)}, bf16[2,512,896]{1,2,0:T(8,128)(2,1)}, u32[]{:S(2)}, u32[]{:S(2)}) collective-permute-start(bf16[2,512,896]{1,2,0:T(8,128)(2,1)} %maximum_maximum_fusion), channel_id=1, source_target_pairs={{0,32},{8,40},{16,48},{24,56},{32,64},{40,72},{48,80},{56,88},{64,... | collective-permute-start | bytes 5505032 | tf_op jit(solution)/shard_map/ppermute | solution.py:34
  142.0 0.7 copy-start.7
  142.6 1.0 copy-start.1
  142.6 1.0 copy-start.5
  144.2 0.7 copy-start.14
  144.9 0.8 copy-start.11
  159.5 41.4 %copy-start.15 = (f32[896]{0:T(1024)S(1)}, f32[896]{0:T(1024)}, u32[]{:S(2)}) copy-start(f32[896]{0:T(1024)} %param.15) | copy-start | bytes 10756
  217.6 0.7 copy-start.17
  217.6 142.8 %all-gather.2.cloned.1.call-start = ((), (), s32[]{:S(2)}) async-start(), calls=%async_computation.5 | async-start | bytes 4423680 | tf_op jit(solution)/shard_map/all_gather | solution.py:174
  368.0 7.9 %copy-start.12 = (f32[128,8]{0,1:T(8,128)S(1)}, f32[128,8]{0,1:T(8,128)}, u32[]{:S(2)}) copy-start(f32[128,8]{0,1:T(8,128)} %param.17) | copy-start | bytes 12292
  368.0 38.7 %all-to-all-start.2 = ((bf16[32,40,896]{2,1,0:T(8,128)(2,1)}), bf16[32,40,896]{2,1,0:T(8,128)(2,1)}, u32[]{:S(2)}, u32[]{:S(2)}) async-start(bf16[32,40,896]{2,1,0:T(8,128)(2,1)} %bitcast.231), calls=%async_computation.3 | async-start | bytes 4587520 | tf_op jit(solution)/shard_map/all_to_all | solution.py:179
Sparse Core Ops, SparseCore 0:
  217.8 89.5 reduce-scatter.1
  309.9 50.5 all-gather.1
where the time goes:
time: 427 us; the launch traced here: 424 us
  waiting for transfers between devices  181 us (42%)
  blocking collectives  70.6 us (17%)
  local copies, waits for them, and re-layouts  49.8 us (12%)
  other arithmetic  46.3 us (11%)
  matrix products  31.9 us (7%)
  starting transfers between devices  30.4 us (7%)
  between operations  13.8 us (3%)
    reduce_scatter x1, waiting for transfers between devices, local(): lax.psum_scatter(partials.astype(jnp.bfloat16), 'exp', scatter_dimension=...  58.5 us
    all_gather x1, waiting for transfers between devices, local(): lax.all_gather(activated, 'exp', axis=1, tiled=True)  50.7 us
    ppermute x3, waiting for transfers between devices, passed_along(): return lax.ppermute(shard, axis, pairs)  41.5 us
    all_to_all x1, blocking collectives, local(): lax.all_to_all(outgoing, 'seq', split_axis=0, concat_axis=0, tiled=True)  41.4 us
    all_to_all x1, waiting for transfers between devices, local(): lax.all_to_all(results_here, 'seq', split_axis=0, concat_axis=0, tiled=True)  30.6 us
    unnamed x1, blocking collectives  29.2 us
    dot_general x1, matrix products, local(): jnp.einsum('rd,dgh->rgh', normed, w_gate_up[0], preferred_element_type=jn...  16 us
    another operation x2, other arithmetic  15.6 us
  transfers between devices with their start and end apart: 7, of which 5 were waited for; matrix products, arithmetic and copies ran while one was open for 15% of the time, Pallas kernels for 0%

commit v1 on v0

--- a/solution.py
+++ b/solution.py
@@ -171,7 +171,9 @@
     )
     down_rows = w_down[0]
     result = jnp.dot(
-        lax.all_gather(activated, "exp", axis=1, tiled=True),
+        jnp.concatenate(
+            lax.all_to_all(jnp.stack([activated] * lax.axis_size("exp")), "exp", 0, 0), axis=1
+        ),
         down_rows,
         preferred_element_type=jnp.float32,
     )

time: 427 us -> 468 us (1.096)
  blocking collectives: 70.6 us -> 163 us
  waiting for transfers between devices: 181 us -> 131 us
    all_to_all x0 -> x1, blocking collectives: none -> 92.6 us  [local(): lax.all_to_all(jnp.stack([activated] * lax.axis_size('exp')), 'exp', 0, 0)]
    all_gather x1 -> x0, waiting for transfers between devices: 50.7 us -> none  [local(): lax.all_gather(activated, 'exp', axis=1, tiled=True)]
  transfers between devices with their start and end apart: 7 -> 6, of which waited for: 5 -> 4; matrix products, arithmetic and copies ran while one was open for 15% -> 14% of each run, Pallas kernels for 0% -> 0%
where the time goes in v1:
time: 468 us; the launch traced here: 465 us
  blocking collectives  163 us (35%)
  waiting for transfers between devices  131 us (28%)
  local copies, waits for them, and re-layouts  50.2 us (11%)
  other arithmetic  45.5 us (10%)
  starting transfers between devices  31.9 us (7%)
  matrix products  29.8 us (6%)
  between operations  13.8 us (3%)
    all_to_all x1, blocking collectives, local(): lax.all_to_all(jnp.stack([activated] * lax.axis_size('exp')), 'exp', 0, 0)  92.6 us
    reduce_scatter x1, waiting for transfers between devices, local(): lax.psum_scatter(partials.astype(jnp.bfloat16), 'exp', scatter_dimension=...  58.5 us
    ppermute x3, waiting for transfers between devices, passed_along(): return lax.ppermute(shard, axis, pairs)  41.5 us
    all_to_all x1, blocking collectives, local(): lax.all_to_all(outgoing, 'seq', split_axis=0, concat_axis=0, tiled=True)  41.4 us
    all_to_all x1, waiting for transfers between devices, local(): lax.all_to_all(results_here, 'seq', split_axis=0, concat_axis=0, tiled=True)  30.6 us
    unnamed x1, blocking collectives  29.2 us
    dot_general x1, matrix products, local(): jnp.einsum('rd,dgh->rgh', normed, w_gate_up[0], preferred_element_type=jn...  16 us
    another operation x2, other arithmetic  15.6 us
  transfers between devices with their start and end apart: 6, of which 4 were waited for; matrix products, arithmetic and copies ran while one was open for 14% of the time, Pallas kernels for 0%

profile of v1, /device:TPU:1, one launch (start us, length us, event | category | flops | bytes accessed | tf_op | source)
XLA Modules:
  0.0 465.1 jit_solution(17120051237919265335)
XLA Ops:
  6.5 1.2 copy.99
  7.8 1.1 copy.103
  8.9 0.8 pad_maximum_fusion
  9.8 4.5 collective-permute-start
  14.3 1.0 convert_reduce_fusion
  15.3 0.8 broadcast_in_dim.167
  16.1 7.0 %all-to-all-start = ((bf16[32,2,2,896]{3,2,1,0:T(2,128)(2,1)}), bf16[32,2,2,896]{3,2,1,0:T(2,128)(2,1)}, u32[]{:S(2)}, u32[]{:S(2)}) async-start(bf16[32,2,2,896]{3,2,1,0:T(2,128)(2,1)} %broadcast_in_dim.167), calls=%async_computation | async-start | bytes 458752 | tf_op jit(solution)/shard_map/all_to_all | solution.py:17
  24.9 0.7 broadcast_subtract_fusion.2
  26.4 1.3 compare_reduce_fusion
  27.7 1.0 compare_reduce_fusion.1
  30.1 0.7 fusion.62
  30.8 15.6 %reduce-window.6 = s32[32,8,128]{2,1,0:T(8,128)S(1)} reduce-window(s32[32,8,128]{2,1,0:T(8,128)} %fusion.62, s32[]{:T(128)} %constant.123.clone.1), window={size=1x1x128 pad=0_0x0_0x127_0}, to_apply=%region_16.17 | reduce-window | flops 4161536 | bytes 262148 | tf_op jit(solution)/shard_map/reduce-window
  46.4 0.8 slice.70
  47.1 1.0 copy.123
  48.7 0.7 copy.124
  49.5 0.7 add_add_fusion
  50.2 1.2 compare_reduce_fusion.3
  51.5 1.6 compare_and_fusion
  53.1 1.5 compare_and_fusion.1
  54.5 0.8 compare_and_fusion.3
  55.3 1.3 broadcast_multiply_fusion
  56.6 0.7 eq.89
  57.4 1.1 copy.93
  58.5 0.7 copy.98
  59.2 1.0 copy.115
  60.2 0.9 copy.111
  61.1 1.3 copy.158
  62.4 1.3 copy.157
  63.6 1.4 copy.120
  65.0 1.5 mul.243
  66.5 0.9 fusion.61
  67.5 1.3 compare_select_fusion.1
  68.8 2.0 maximum_maximum_fusion.1
  70.8 4.2 collective-permute-start.1
  75.6 1.6 select_reduce_fusion.2
  77.8 1.8 fusion.97
  79.7 1.6 reshape_squeeze.24
  81.3 12.4 %collective-permute-done.1 = bf16[2,256,896]{1,2,0:T(8,128)(2,1)} collective-permute-done((bf16[2,256,896]{1,2,0:T(8,128)(2,1)}, bf16[2,256,896]{1,2,0:T(8,128)(2,1)}, u32[]{:S(2)}, u32[]{:S(2)}) %collective-permute-start.1) | collective-permute-done | bytes 917536 | tf_op jit(solution)/shard_map/ppermute | solution.py:34
  93.7 2.7 maximum_maximum_fusion
  96.4 6.8 %collective-permute-start.2 = (bf16[2,512,896]{1,2,0:T(8,128)(2,1)}, bf16[2,512,896]{1,2,0:T(8,128)(2,1)}, u32[]{:S(2)}, u32[]{:S(2)}) collective-permute-start(bf16[2,512,896]{1,2,0:T(8,128)(2,1)} %maximum_maximum_fusion), channel_id=1, source_target_pairs={{0,32},{8,40},{16,48},{24,56},{32,64},{40,72},{48,80},{56,88},{64,... | collective-permute-start | bytes 5505032 | tf_op jit(solution)/shard_map/ppermute | solution.py:34
  103.2 0.8 select_reduce_fusion.3
  104.1 1.6 reshape_squeeze.25
  105.7 0.7 compare_select_fusion.2
  106.4 0.7 fusion.58
  107.1 1.2 fusion.24
  108.3 1.1 fusion.96
  109.7 1.2 fusion.95
  111.3 29.2 %collective-permute-done.2 = bf16[2,512,896]{1,2,0:T(8,128)(2,1)} collective-permute-done((bf16[2,512,896]{1,2,0:T(8,128)(2,1)}, bf16[2,512,896]{1,2,0:T(8,128)(2,1)}, u32[]{:S(2)}, u32[]{:S(2)}) %collective-permute-start.2) | collective-permute-done | bytes 1835040 | tf_op jit(solution)/shard_map/ppermute | solution.py:34
  140.4 1.6 fusion.94
  145.7 13.9 %scatter_custom_fusion = bf16[1280,896]{1,0:T(8,128)(2,1)} fusion(s32[1024]{0:T(1024)S(1)} %bitcast.251, bf16[128,896]{1,0:T(8,128)(2,1)S(1)} %copy.119, s32[1024]{0:T(1024)} %broadcast_clamp_fusion.1, bf16[]{:T(256)} %constant.138.clone.1), kind=kCustom, calls=%fused_computation.20 | custom fusion | bytes 2294272 | tf_op jit(solution)/shard_map/scatter | solution.py:151
  159.5 41.4 %all_to_all.20 = bf16[32,40,896]{2,1,0:T(8,128)(2,1)S(1)} all-to-all(bf16[32,40,896]{2,1,0:T(8,128)(2,1)} %bitcast.219), channel_id=1, replica_groups=mesh['seq'=32,'exp'=8] {'seq'}, dimensions={0} | all-to-all | bytes 4587520 | tf_op jit(solution)/shard_map/all_to_all | solution.py:154
  200.9 0.8 fusion.2
  201.6 16.0 %convolution_convert_fusion = bf16[1280,2,1536]{0,2,1:T(8,128)(2,1)} fusion(bf16[1280,896,1]{1,0,2:T(8,128)(2,1)S(1)} %bitcast.236, bf16[896,2,1536]{2,1,0:T(2,128)(2,1)} %bitcast.256), kind=kOutput, calls=%fused_computation.3 | convolution fusion | flops 7050362880 | bytes 15663104 | tf_op jit(solution)/shard_map/rd,dgh->rgh/dot_general | solution.py:160
  219.0 29.2 %all-reduce = bf16[1280,8]{0,1:T(8,128)(2,1)S(1)} all-reduce(bf16[1280,8]{0,1:T(8,128)(2,1)S(1)} %broadcast_in_dim.186), channel_id=3, replica_groups=mesh['seq'=32,'exp'=8] {'exp'}, use_global_device_ids=true, to_apply=%region_22.23.clone | all-reduce | flops 10240 | bytes 40960
  248.2 0.7 rsqrt_reduce_fusion
  248.8 58.5 %reduce-scatter.2.cloned.1.call-done = bf16[1280,2,192]{0,2,1:T(8,128)(2,1)} async-done(((bf16[1280,2,1536]{0,2,1:T(8,128)(2,1)}), bf16[1280,2,192]{0,2,1:T(8,128)(2,1)}) %reduce-scatter.2.cloned.1.call-update) | async-done | bytes 983056 | tf_op jit(solution)/shard_map/reduce_scatter | solution.py:162
  307.4 1.3 convert_element_type.90
  309.3 92.6 %all_to_all.21 = bf16[8,1280,192]{1,2,0:T(8,128)(2,1)S(1)} all-to-all(bf16[8,1280,192]{1,2,0:T(8,128)(2,1)S(1)} %stack.32), channel_id=1, replica_groups=mesh['seq'=32,'exp'=8] {'exp'}, dimensions={0} | all-to-all | bytes 7864320 | tf_op jit(solution)/shard_map/all_to_all | solution.py:175
  401.9 5.5 %convolution_convert_fusion.1 = bf16[1280,896]{1,0:T(8,128)(2,1)} fusion(bf16[1280,1536]{0,1:T(8,128)(2,1)S(1)} %bitcast.233, bf16[1,1536,896]{2,1,0:T(8,128)(2,1)S(1)} %copy-done), kind=kOutput, calls=%fused_computation.9 | convolution fusion | flops 3524362240 | bytes 8978432 | tf_op jit(solution)/shard_map/dot_general | solution.py:173
  407.4 9.4 %all-to-all-start.3 = ((bf16[32,40,896]{2,1,0:T(8,128)(2,1)}), bf16[32,40,896]{2,1,0:T(8,128)(2,1)}, u32[]{:S(2)}, u32[]{:S(2)}) async-start(bf16[32,40,896]{2,1,0:T(8,128)(2,1)} %bitcast.235), calls=%async_computation.4 | async-start | bytes 4587520 | tf_op jit(solution)/shard_map/all_to_all | solution.py:181
  417.0 30.6 %all-to-all-done.3 = bf16[32,40,896]{2,1,0:T(8,128)(2,1)} async-done(((bf16[32,40,896]{2,1,0:T(8,128)(2,1)}), bf16[32,40,896]{2,1,0:T(8,128)(2,1)}, u32[]{:S(2)}, u32[]{:S(2)}) %all-to-all-start.3) | async-done | bytes 2293792 | tf_op jit(solution)/shard_map/all_to_all | solution.py:181
  447.7 7.7 %gather_fusion = bf16[1024,896]{1,0:T(8,128)(2,1)} fusion(bf16[1280,896]{1,0:T(8,128)(2,1)} %bitcast.52, s32[1024]{0:T(1024)S(1)} %broadcast_clamp_fusion), kind=kCustom, calls=%fused_computation.1 | custom fusion | bytes 3674112 | tf_op jit(solution)/shard_map/gather | solution.py:183
  455.4 2.2 fusion.4
  457.6 0.7 fusion.42
  (86 shorter events, 12.2 us)
Async XLA Ops:
  6.5 395.4 %copy-start = (bf16[1,1536,896]{2,1,0:T(8,128)(2,1)S(1)}, bf16[1,1536,896]{2,1,0:T(8,128)(2,1)}, u32[]{:S(2)}) copy-start(bf16[1,1536,896]{2,1,0:T(8,128)(2,1)} %param.19) | copy-start | bytes 8257540
  6.5 7.7 %copy-start.2 = (bf16[128,896]{1,0:T(8,128)(2,1)S(1)}, bf16[128,896]{1,0:T(8,128)(2,1)}, u32[]{:S(2)}) copy-start(bf16[128,896]{1,0:T(8,128)(2,1)} %param.12) | copy-start | bytes 688132
  6.5 19.8 %copy-start.16 = (s32[2,8]{1,0:T(2,128)S(1)}, s32[2,8]{1,0:T(2,128)}, u32[]{:S(2)}) copy-start(s32[2,8]{1,0:T(2,128)} %param.14) | copy-start | bytes 196
  7.8 21.5 %copy-start.13 = (f32[128,2,7]{0,1,2:T(2,128)S(1)}, f32[128,2,7]{0,1,2:T(2,128)}, u32[]{:S(2)}) copy-start(f32[128,2,7]{0,1,2:T(2,128)} %param.13) | copy-start | bytes 21508
  7.8 22.1 %copy-start.10 = (s32[128,8]{0,1:T(8,128)S(1)}, s32[128,8]{0,1:T(8,128)}, u32[]{:S(2)}) copy-start(s32[128,8]{0,1:T(8,128)} %param.16) | copy-start | bytes 12292
  9.8 59.0 %collective-permute-start = (bf16[2,128,896]{1,2,0:T(8,128)(2,1)}, bf16[2,128,896]{1,2,0:T(8,128)(2,1)}, u32[]{:S(2)}, u32[]{:S(2)}) collective-permute-start(bf16[2,128,896]{1,2,0:T(8,128)(2,1)} %pad_maximum_fusion), channel_id=1, source_target_pairs={{0,8},{8,16},{16,24},{24,32},{32,40},{40,48},{48,56},{56,64},{64,7... | collective-permute-start | bytes 1376264 | tf_op jit(solution)/shard_map/ppermute | solution.py:34
  16.1 61.7 %all-to-all-start = ((bf16[32,2,2,896]{3,2,1,0:T(2,128)(2,1)}), bf16[32,2,2,896]{3,2,1,0:T(2,128)(2,1)}, u32[]{:S(2)}, u32[]{:S(2)}) async-start(bf16[32,2,2,896]{3,2,1,0:T(2,128)(2,1)} %broadcast_in_dim.167), calls=%async_computation | async-start | bytes 458752 | tf_op jit(solution)/shard_map/all_to_all | solution.py:17
  23.1 284.3 %reduce-scatter.2.cloned.1.call-start = ((), (), s32[]{:S(2)}) async-start(), calls=%async_computation.5 | async-start | bytes 8847360 | tf_op jit(solution)/shard_map/reduce_scatter | solution.py:162
  23.2 3.1 copy-start.8
  66.5 8.5 %copy-start.9 = (s32[128]{0:T(128)S(1)}, s32[128]{0:T(128)}, u32[]{:S(2)}) copy-start(s32[128]{0:T(128)} %copy-done.8) | copy-start | bytes 1540
  66.5 9.1 %copy-start.4 = (pred[128,128]{0,1:T(8,128)(4,1)S(1)}, pred[128,128]{0,1:T(8,128)(4,1)}, u32[]{:S(2)}) copy-start(pred[128,128]{0,1:T(8,128)(4,1)} %copy.98) | copy-start | bytes 49156
  70.8 22.9 %collective-permute-start.1 = (bf16[2,256,896]{1,2,0:T(8,128)(2,1)}, bf16[2,256,896]{1,2,0:T(8,128)(2,1)}, u32[]{:S(2)}, u32[]{:S(2)}) collective-permute-start(bf16[2,256,896]{1,2,0:T(8,128)(2,1)} %maximum_maximum_fusion.1), channel_id=1, source_target_pairs={{0,16},{8,24},{16,32},{24,40},{32,48},{40,56},{48,64},{56,72},{64,... | collective-permute-start | bytes 2752520 | tf_op jit(solution)/shard_map/ppermute | solution.py:34
  81.3 21.9 %copy-start.3 = (bf16[64,7,128]{2,1,0:T(8,128)(2,1)S(1)}, bf16[64,7,128]{2,1,0:T(8,128)(2,1)}, u32[]{:S(2)}) copy-start(bf16[64,7,128]{2,1,0:T(8,128)(2,1)} %reshape_squeeze.24) | copy-start | bytes 344068
  81.3 21.9 %copy-start.6 = (pred[128,64]{0,1:T(8,128)(4,1)S(1)}, pred[128,64]{0,1:T(8,128)(4,1)}, u32[]{:S(2)}) copy-start(pred[128,64]{0,1:T(8,128)(4,1)} %iota_compare_fusion.2) | copy-start | bytes 24580
  96.4 44.0 %collective-permute-start.2 = (bf16[2,512,896]{1,2,0:T(8,128)(2,1)}, bf16[2,512,896]{1,2,0:T(8,128)(2,1)}, u32[]{:S(2)}, u32[]{:S(2)}) collective-permute-start(bf16[2,512,896]{1,2,0:T(8,128)(2,1)} %maximum_maximum_fusion), channel_id=1, source_target_pairs={{0,32},{8,40},{16,48},{24,56},{32,64},{40,72},{48,80},{56,88},{64,... | collective-permute-start | bytes 5505032 | tf_op jit(solution)/shard_map/ppermute | solution.py:34
  142.0 0.7 copy-start.7
  142.6 1.0 copy-start.1
  142.6 1.0 copy-start.5
  144.2 0.7 copy-start.14
  144.9 0.8 copy-start.11
  159.5 41.4 %copy-start.15 = (f32[896]{0:T(1024)S(1)}, f32[896]{0:T(1024)}, u32[]{:S(2)}) copy-start(f32[896]{0:T(1024)} %param.15) | copy-start | bytes 10756
  217.6 0.7 copy-start.17
  407.4 9.4 %copy-start.12 = (f32[128,8]{0,1:T(8,128)S(1)}, f32[128,8]{0,1:T(8,128)}, u32[]{:S(2)}) copy-start(f32[128,8]{0,1:T(8,128)} %param.17) | copy-start | bytes 12292
  407.4 40.3 %all-to-all-start.3 = ((bf16[32,40,896]{2,1,0:T(8,128)(2,1)}), bf16[32,40,896]{2,1,0:T(8,128)(2,1)}, u32[]{:S(2)}, u32[]{:S(2)}) async-start(bf16[32,40,896]{2,1,0:T(8,128)(2,1)} %bitcast.235), calls=%async_computation.4 | async-start | bytes 4587520 | tf_op jit(solution)/shard_map/all_to_all | solution.py:181
Sparse Core Ops, SparseCore 0:
  217.8 89.5 reduce-scatter.1
